TPU v7x, 32 devices: a whole 2x2x4 slice. The times are simulated.
32 devices in a mesh: grp: 2 (over y), cls: 8 (over z, x), img: 2 (over core).
Axes of the slice: x: 2, y: 2, z: 4, core: 2. Of those that a mesh axis runs over, the one named last changes fastest.
Arguments:
- embeddings: bfloat16 [4096, 1536], P(('grp', 'img'), 'cls'), parts along dimension 0, may hold values from -6 to 6, as said below
- labels: int32 [4096], P(('grp', 'img')), parts along dimension 0, may hold values from 0 to 1023
- weights: float32 [3072, 1024], P(('grp', 'img'), 'cls'), parts along dimension 0, may hold values from -12 to 12, as said below
- strength: int32 [2], P('grp'), parts along dimension 0, may hold values from 0 to 3
Outputs:
- new_weights: float32 [3072, 1024], P(('grp', 'img'), 'cls'), parts along dimension 0
- losses: float32 [4096], P(('grp', 'img')), parts along dimension 0
There are 2 independent parts, one for each index of `grp`. A program takes and returns all parts, laid end to end along the dimension named above; each array names one. Nothing has to cross between parts.
Inputs may be any that keep to these rules, and one draw needn't show every extreme that they name: embeddings of order one. Initial probe weights of order a few.
All inputs are finite; a program needn't handle non-finite values.
Results may differ from a plain program's by a relative error of at most 0.0032.
Values may be sent and summed in bfloat16 or wider, within the bound.
A program may use at most 64 MiB of HBM per device.

v0:
```python
import math
import jax
import jax.numpy as jnp
from jax import lax
from jax.sharding import PartitionSpec as P

D = 1536
ITERS = 2


def shrink(master, grad, lam):
    moved = master - 16.0 * grad
    return jnp.sign(moved) * jnp.maximum(jnp.abs(moved) - lam, 0.0)


def shards(embeddings, labels, weights, strength):
    scale = 1.0 / math.sqrt(D)
    lam = 16.0 * 0.01 * jnp.exp2(strength[0].astype(jnp.float32))
    full_x = lax.all_gather(embeddings, "cls", axis=1, tiled=True)
    cls_width = weights.shape[1]
    first_class = lax.axis_index("cls") * cls_width
    classes = first_class + lax.iota(jnp.int32, cls_width)
    onehot = (labels[:, None] == classes[None, :]).astype(jnp.float32)
    master = lax.all_gather(weights, "img", axis=0, tiled=True)
    operand = master.astype(jnp.bfloat16)
    losses = jnp.zeros((labels.shape[0],), jnp.float32)
    for step in range(ITERS):
        logits = jnp.dot(full_x, operand, preferred_element_type=jnp.float32) * scale
        local_top = jnp.max(logits, axis=1)
        label_term = jnp.sum(logits * onehot, axis=1)
        top = lax.pmax(local_top, "cls")
        total, picked = lax.psum(
            (jnp.sum(jnp.exp(logits - top[:, None]), axis=1), label_term), "cls"
        )
        lse = top + jnp.log(total)
        losses = lse - picked
        resid = (jnp.exp(logits - lse[:, None]) - onehot).astype(jnp.bfloat16)
        grad_local = (
            lax.dot_general(
                full_x, resid, (((0,), (0,)), ((), ())), preferred_element_type=jnp.float32
            )
            * scale
        )
        grad = lax.psum(grad_local, "img")
        master = shrink(master, grad, lam)
        operand = master.astype(jnp.bfloat16)
    rows = weights.shape[0]
    new_weights = lax.dynamic_slice_in_dim(master, lax.axis_index("img") * rows, rows, 0)
    return (new_weights, losses)


def solution(mesh):
    placed = (P(("grp", "img"), "cls"), P(("grp", "img")), P(("grp", "img"), "cls"), P("grp"))
    return jax.shard_map(
        shards,
        mesh=mesh,
        in_specs=placed,
        out_specs=(P(("grp", "img"), "cls"), P(("grp", "img"))),
        check_vma=False,
    )
```

profile of v0, /device:TPU:0, one launch (start us, length us, event | category | flops | bytes accessed | tf_op | source)
XLA Modules:
  0.0 210.3 jit_solution(16586278713644996422)
XLA Ops:
  7.2 0.0 all-gather.2.cloned.1.call-start
  7.2 0.7 all-gather.2.cloned.1.call-update
  7.9 0.0 all-reduce.4.cloned.1.call-start
  7.9 1.2 copy.6
  9.1 2.6 %all_gather.6 = f32[1536,128]{0,1:T(8,128)} all-gather(f32[768,128]{0,1:T(8,128)S(1)} %copy.6), channel_id=1, replica_groups=mesh['grp'=2,'cls'=8,'img'=2] {'img'}, dimensions={0}, use_global_device_ids=true | all-gather | bytes 1179648 | tf_op jit(solution)/shard_map/all_gather | solution.py:24
  11.7 61.6 %all-gather.2.cloned.1.call-done = bf16[1024,1536]{0,1:T(8,128)(2,1)} async-done(((bf16[1024,192]{0,1:T(8,128)(2,1)}), bf16[1024,1536]{0,1:T(8,128)(2,1)}) %all-gather.2.cloned.1.call-update) | async-done | bytes 3145744 | tf_op jit(solution)/shard_map/all_gather | solution.py:19
  73.4 3.7 %fusion.19 = (f32[1024]{0:T(1024)S(1)}, f32[1024,128]{0,1:T(8,128)}) fusion(bf16[1024,1536]{0,1:T(8,128)(2,1)} %all-gather.2.cloned.1.call-done, f32[1536,128]{0,1:T(8,128)} %all_gather.6), kind=kOutput, calls=%fused_computation.34 | convolution fusion | flops 403110912 | bytes 4460544 | tf_op jit(solution)/shard_map/dot_general | solution.py:28
  77.0 19.0 %pmax.14 = f32[1024]{0:T(1024)S(1)} all-reduce(f32[1024]{0:T(1024)S(1)} %get-tuple-element.10), channel_id=1, replica_groups=mesh['grp'=2,'cls'=8,'img'=2] {'cls'}, use_global_device_ids=true, to_apply=%region_1.0 | all-reduce | flops 1024 | bytes 8192 | tf_op jit(solution)/shard_map/pmax | solution.py:31
  96.1 1.1 exponential_reduce_fusion
  97.2 17.2 %psum.35 = f32[1024]{0:T(1024)S(1)} all-reduce(f32[1024]{0:T(1024)S(1)} %exponential_reduce_fusion), channel_id=1, replica_groups=mesh['grp'=2,'cls'=8,'img'=2] {'cls'}, use_global_device_ids=true, to_apply=%region_3.0 | all-reduce | flops 1024 | bytes 8192 | tf_op jit(solution)/shard_map/psum | solution.py:32
  114.4 3.1 %fusion = f32[1536,128]{0,1:T(8,128)} fusion(bf16[1024,1536]{0,1:T(8,128)(2,1)S(1)} %copy-done, f32[1024,128]{0,1:T(8,128)} %get-tuple-element.11, s32[1024]{0:T(1024)S(1)} %copy-done.2, f32[1024]{0:T(1024)S(1)} %log_add_fusion.1, s32[128]{0:T(128)S(1)} %iota_add_fusion), kind=kOutput, calls=%fused_computation.2 | convolution fusion | flops 403505152 | bytes 4465152 | tf_op jit(solution)/shard_map/dot_general | solution.py:39
  117.6 0.0 all-reduce.6.cloned.1.call-start
  118.3 17.2 %all-reduce.4.cloned.1.call-done = f32[1536,128]{0,1:T(8,128)} async-done(((f32[1536,128]{0,1:T(8,128)}), f32[1536,128]{0,1:T(8,128)}) %all-reduce.4.cloned.1.call-update) | async-done | bytes 786448 | tf_op jit(solution)/shard_map/psum | solution.py:44
  135.6 1.7 maximum_multiply_fusion
  137.3 0.9 copy-done.1
  138.2 1.4 fusion.20
  139.5 21.6 %pmax.15 = f32[1024]{0:T(1024)S(1)} all-reduce(f32[1024]{0:T(1024)S(1)} %get-tuple-element.12), channel_id=1, replica_groups=mesh['grp'=2,'cls'=8,'img'=2] {'cls'}, use_global_device_ids=true, to_apply=%region_6.0 | all-reduce | flops 1024 | bytes 8192 | tf_op jit(solution)/shard_map/pmax | solution.py:31
  161.2 1.2 fusion.2
  162.3 17.4 %all-reduce = (f32[1024]{0:T(1024)S(1)}, f32[1024]{0:T(1024)S(1)}) all-reduce(f32[1024]{0:T(1024)S(1)} %get-tuple-element.5, f32[1024]{0:T(1024)S(1)} %get-tuple-element.4), channel_id=1, replica_groups=mesh['grp'=2,'cls'=8,'img'=2] {'cls'}, use_global_device_ids=true, to_apply=%region_8.0 | all-reduce | flops 2048 | bytes 16384 | tf_op jit(solution)/shard_map/psum | solution.py:32
  179.7 0.6 fusion.18
  180.3 3.1 %fusion.1 = f32[1536,128]{0,1:T(8,128)} fusion(bf16[1024,1536]{0,1:T(8,128)(2,1)S(1)} %copy-done, f32[128,1024]{1,0:T(8,128)} %get-tuple-element.13, f32[1024]{0:T(1024)S(1)} %get-tuple-element.9, s32[1024]{0:T(1024)S(1)} %copy-done.2, s32[128]{0:T(128)S(1)} %iota_add_fusion), kind=kOutput, calls=%fused_computation.3 | convolution fusion | flops 403505152 | bytes 4465152 | tf_op jit(solution)/shard_map/dot_general | solution.py:39
  183.5 18.1 %all-reduce.6.cloned.1.call-done = f32[1536,128]{0,1:T(8,128)} async-done(((f32[1536,128]{0,1:T(8,128)}), f32[1536,128]{0,1:T(8,128)}) %all-reduce.6.cloned.1.call-update) | async-done | bytes 786448 | tf_op jit(solution)/shard_map/psum | solution.py:44
  201.5 1.3 maximum_multiply_fusion.1
  202.8 0.9 copy.7
  (9 shorter events, 0.1 us)
Async XLA Ops:
  7.2 66.2 %all-gather.2.cloned.1.call-start = ((), (), s32[]{:S(2)}) async-start(), calls=%async_computation | async-start | bytes 3538944 | tf_op jit(solution)/shard_map/all_gather | solution.py:19
  7.9 127.7 %all-reduce.4.cloned.1.call-start = ((), (), s32[]{:S(2)}) async-start(), calls=%async_computation.1 | async-start | bytes 1572864 | tf_op jit(solution)/shard_map/psum | solution.py:44
  9.1 105.3 %copy-start.2 = (s32[1024]{0:T(1024)S(1)}, s32[1024]{0:T(1024)}, u32[]{:S(2)}) copy-start(s32[1024]{0:T(1024)} %param.5) | copy-start | bytes 12292
  73.4 41.1 %copy-start = (bf16[1024,1536]{0,1:T(8,128)(2,1)S(1)}, bf16[1024,1536]{0,1:T(8,128)(2,1)}, u32[]{:S(2)}) copy-start(bf16[1024,1536]{0,1:T(8,128)(2,1)} %all-gather.2.cloned.1.call-done) | copy-start | bytes 9437188
  117.6 83.9 %all-reduce.6.cloned.1.call-start = ((), (), s32[]{:S(2)}) async-start(), calls=%async_computation.2 | async-start | bytes 1572864 | tf_op jit(solution)/shard_map/psum | solution.py:44
  137.3 0.9 copy-start.1
Sparse Core Ops, SparseCore 0:
  10.2 63.1 all-gather.1
  117.7 17.8 all-reduce.3
  183.6 17.8 all-reduce.5
where the time goes:
time: 211 us; the launch traced here: 210 us
  waiting for transfers between devices  97.6 us (46%)
  blocking collectives  77.8 us (37%)
  between operations  14.5 us (7%)
  matrix products  11.3 us (5%)
  other arithmetic  5.92 us (3%)
  local copies, waits for them, and re-layouts  2.95 us (1%)
    all_gather x1, waiting for transfers between devices, shards(): full_x = lax.all_gather(embeddings, 'cls', axis=1, tiled=True)  61.6 us
    pmax x2, blocking collectives, shards(): top = lax.pmax(local_top, 'cls')  40.6 us
    psum x2, waiting for transfers between devices, shards(): grad = lax.psum(grad_local, 'img')  35.3 us
    psum x2, blocking collectives, shards(): lax.psum((jnp.sum(jnp.exp(logits - top[:, None]), axis=1), label_term), '...  34.6 us
    dot_general x2, matrix products, shards(): lax.dot_general(full_x, resid, (((0,), (0,)), ((), ())), preferred_elemen...  6.27 us
    dot_general x2, matrix products, shards(): jnp.dot(full_x, operand, preferred_element_type=jnp.float32) * scale  5.05 us
  transfers between devices with their start and end apart: 3, of which 3 were waited for; matrix products, arithmetic and copies ran while one was open for 1% of the time, Pallas kernels for 0%

commit v1 on v0

--- a/solution.py
+++ b/solution.py
@@ -41,7 +41,7 @@
             )
             * scale
         )
-        grad = lax.psum(grad_local, "img")
+        grad = lax.all_gather(grad_local, "img").sum(axis=0)
         master = shrink(master, grad, lam)
         operand = master.astype(jnp.bfloat16)
     rows = weights.shape[0]

time: 211 us -> 203 us (0.962)
  waiting for transfers between devices: 97.6 us -> 78.8 us
  local copies, waits for them, and re-layouts: 2.95 us -> 9.03 us
  other arithmetic: 5.92 us -> 10.8 us
    psum x2 -> x0, waiting for transfers between devices: 35.3 us -> none  [shards(): grad = lax.psum(grad_local, 'img')]
    all_gather x0 -> x2, waiting for transfers between devices: none -> 16.5 us  [shards(): grad = lax.all_gather(grad_local, 'img').sum(axis=0)]
    all_gather x0 -> x2, local copies, waits for them, and re-layouts: none -> 6.07 us  [shards(): grad = lax.all_gather(grad_local, 'img').sum(axis=0)]
    reduce_sum x0 -> x2, other arithmetic: none -> 6.02 us  [shards(): grad = lax.all_gather(grad_local, 'img').sum(axis=0)]
where the time goes in v1:
time: 203 us; the launch traced here: 202 us
  waiting for transfers between devices  78.8 us (39%)
  blocking collectives  77.8 us (38%)
  between operations  14.5 us (7%)
  matrix products  11.3 us (6%)
  other arithmetic  10.8 us (5%)
  local copies, waits for them, and re-layouts  9.03 us (4%)
    all_gather x1, waiting for transfers between devices, shards(): full_x = lax.all_gather(embeddings, 'cls', axis=1, tiled=True)  61.6 us
    pmax x2, blocking collectives, shards(): top = lax.pmax(local_top, 'cls')  40.6 us
    psum x2, blocking collectives, shards(): lax.psum((jnp.sum(jnp.exp(logits - top[:, None]), axis=1), label_term), '...  34.6 us
    all_gather x2, waiting for transfers between devices, shards(): grad = lax.all_gather(grad_local, 'img').sum(axis=0)  16.5 us
    dot_general x2, matrix products, shards(): lax.dot_general(full_x, resid, (((0,), (0,)), ((), ())), preferred_elemen...  6.25 us
    all_gather x2, local copies, waits for them, and re-layouts, shards(): grad = lax.all_gather(grad_local, 'img').sum(axis=0)  6.07 us
    reduce_sum x2, other arithmetic, shards(): grad = lax.all_gather(grad_local, 'img').sum(axis=0)  6.02 us
    dot_general x2, matrix products, shards(): jnp.dot(full_x, operand, preferred_element_type=jnp.float32) * scale  5.04 us
  transfers between devices with their start and end apart: 3, of which 3 were waited for; matrix products, arithmetic and copies ran while one was open for 1% of the time, Pallas kernels for 0%

profile of v1, /device:TPU:0, one launch (start us, length us, event | category | flops | bytes accessed | tf_op | source)
XLA Modules:
  0.0 202.4 jit_solution(1376812383107186998)
XLA Ops:
  7.2 0.7 all-gather.6.cloned.1.call-update
  7.9 1.2 copy.6
  9.1 2.6 %all_gather.18 = f32[1536,128]{0,1:T(8,128)} all-gather(f32[768,128]{0,1:T(8,128)S(1)} %copy.6), channel_id=1, replica_groups=mesh['grp'=2,'cls'=8,'img'=2] {'img'}, dimensions={0}, use_global_device_ids=true | all-gather | bytes 1179648 | tf_op jit(solution)/shard_map/all_gather | solution.py:24
  11.7 61.6 %all-gather.6.cloned.1.call-done = bf16[1024,1536]{0,1:T(8,128)(2,1)} async-done(((bf16[1024,192]{0,1:T(8,128)(2,1)}), bf16[1024,1536]{0,1:T(8,128)(2,1)}) %all-gather.6.cloned.1.call-update) | async-done | bytes 3145744 | tf_op jit(solution)/shard_map/all_gather | solution.py:19
  73.4 3.7 %fusion.19 = (f32[1024]{0:T(1024)S(1)}, f32[1024,128]{0,1:T(8,128)}) fusion(bf16[1024,1536]{0,1:T(8,128)(2,1)} %all-gather.6.cloned.1.call-done, f32[1536,128]{0,1:T(8,128)} %all_gather.18), kind=kOutput, calls=%fused_computation.34 | convolution fusion | flops 403110912 | bytes 4460544 | tf_op jit(solution)/shard_map/dot_general | solution.py:28
  77.0 19.0 %pmax.14 = f32[1024]{0:T(1024)S(1)} all-reduce(f32[1024]{0:T(1024)S(1)} %get-tuple-element.10), channel_id=1, replica_groups=mesh['grp'=2,'cls'=8,'img'=2] {'cls'}, use_global_device_ids=true, to_apply=%region_1.0 | all-reduce | flops 1024 | bytes 8192 | tf_op jit(solution)/shard_map/pmax | solution.py:31
  96.1 1.1 exponential_reduce_fusion
  97.2 17.2 %psum.21 = f32[1024]{0:T(1024)S(1)} all-reduce(f32[1024]{0:T(1024)S(1)} %exponential_reduce_fusion), channel_id=1, replica_groups=mesh['grp'=2,'cls'=8,'img'=2] {'cls'}, use_global_device_ids=true, to_apply=%region_3.0 | all-reduce | flops 1024 | bytes 8192 | tf_op jit(solution)/shard_map/psum | solution.py:32
  114.4 3.1 %fusion = f32[1536,128]{0,1:T(8,128)} fusion(bf16[1024,1536]{0,1:T(8,128)(2,1)S(1)} %copy-done, f32[1024,128]{0,1:T(8,128)} %get-tuple-element.11, s32[1024]{0:T(1024)S(1)} %copy-done.3, f32[1024]{0:T(1024)S(1)} %log_add_fusion.1, s32[128]{0:T(128)S(1)} %iota_add_fusion), kind=kOutput, calls=%fused_computation.2 | convolution fusion | flops 403505152 | bytes 4465152 | tf_op jit(solution)/shard_map/dot_general | solution.py:39
  118.3 7.8 %all-gather.8.cloned.1.call-done = f32[3072,128]{0,1:T(8,128)} async-done(((f32[1536,128]{0,1:T(8,128)}), f32[3072,128]{0,1:T(8,128)}) %all-gather.8.cloned.1.call-update) | async-done | bytes 1572880 | tf_op jit(solution)/shard_map/all_gather | solution.py:44
  126.1 3.4 %reshape.19 = f32[2,1536,128]{1,0,2:T(2,128)} reshape(f32[3072,128]{0,1:T(8,128)} %all-gather.8.cloned.1.call-done) | data formatting | bytes 3145728 | tf_op jit(solution)/shard_map/all_gather | solution.py:44
  129.6 4.2 %reduce_sum.46 = f32[1536,128]{0,1:T(8,128)} reduce(f32[2,1536,128]{1,0,2:T(2,128)} %reshape.19, f32[]{:T(128)} %constant.14.clone.1), dimensions={0}, to_apply=%region_4.0 | reduce | flops 196608 | bytes 2359300 | tf_op jit(solution)/shard_map/reduce_sum | solution.py:44
  133.7 1.7 maximum_multiply_fusion
  135.4 0.9 copy-done.1
  136.3 1.4 fusion.20
  137.7 21.6 %pmax.15 = f32[1024]{0:T(1024)S(1)} all-reduce(f32[1024]{0:T(1024)S(1)} %get-tuple-element.12), channel_id=1, replica_groups=mesh['grp'=2,'cls'=8,'img'=2] {'cls'}, use_global_device_ids=true, to_apply=%region_6.0 | all-reduce | flops 1024 | bytes 8192 | tf_op jit(solution)/shard_map/pmax | solution.py:31
  159.3 1.2 fusion.2
  160.5 17.4 %all-reduce = (f32[1024]{0:T(1024)S(1)}, f32[1024]{0:T(1024)S(1)}) all-reduce(f32[1024]{0:T(1024)S(1)} %get-tuple-element.5, f32[1024]{0:T(1024)S(1)} %get-tuple-element.4), channel_id=1, replica_groups=mesh['grp'=2,'cls'=8,'img'=2] {'cls'}, use_global_device_ids=true, to_apply=%region_8.0 | all-reduce | flops 2048 | bytes 16384 | tf_op jit(solution)/shard_map/psum | solution.py:32
  177.9 0.6 fusion.18
  178.5 3.1 %fusion.1 = f32[1536,128]{0,1:T(8,128)} fusion(bf16[1024,1536]{0,1:T(8,128)(2,1)S(1)} %copy-done, f32[128,1024]{1,0:T(8,128)} %get-tuple-element.13, f32[1024]{0:T(1024)S(1)} %get-tuple-element.9, s32[1024]{0:T(1024)S(1)} %copy-done.3, s32[128]{0:T(128)S(1)} %iota_add_fusion), kind=kOutput, calls=%fused_computation.3 | convolution fusion | flops 403505152 | bytes 4465152 | tf_op jit(solution)/shard_map/dot_general | solution.py:39
  181.6 8.6 %all-gather.10.cloned.1.call-done = f32[3072,128]{0,1:T(8,128)} async-done(((f32[1536,128]{0,1:T(8,128)}), f32[3072,128]{0,1:T(8,128)}) %all-gather.10.cloned.1.call-update) | async-done | bytes 1572880 | tf_op jit(solution)/shard_map/all_gather | solution.py:44
  190.3 2.6 %reshape.20 = f32[2,1536,128]{1,0,2:T(2,128)S(1)} reshape(f32[3072,128]{0,1:T(8,128)} %all-gather.10.cloned.1.call-done) | data formatting | bytes 3145728 | tf_op jit(solution)/shard_map/all_gather | solution.py:44
  192.9 1.9 reduce_sum.48
  195.0 0.9 copy.7
  (15 shorter events, 0.4 us)
Async XLA Ops:
  7.2 66.2 %all-gather.6.cloned.1.call-start = ((), (), s32[]{:S(2)}) async-start(), calls=%async_computation | async-start | bytes 3538944 | tf_op jit(solution)/shard_map/all_gather | solution.py:19
  7.9 118.2 %all-gather.8.cloned.1.call-start = ((), (), s32[]{:S(2)}) async-start(), calls=%async_computation.1 | async-start | bytes 2359296 | tf_op jit(solution)/shard_map/all_gather | solution.py:44
  9.1 105.3 %copy-start.3 = (s32[1024]{0:T(1024)S(1)}, s32[1024]{0:T(1024)}, u32[]{:S(2)}) copy-start(s32[1024]{0:T(1024)} %param.5) | copy-start | bytes 12292
  73.4 41.1 %copy-start = (bf16[1024,1536]{0,1:T(8,128)(2,1)S(1)}, bf16[1024,1536]{0,1:T(8,128)(2,1)}, u32[]{:S(2)}) copy-start(bf16[1024,1536]{0,1:T(8,128)(2,1)} %all-gather.6.cloned.1.call-done) | copy-start | bytes 9437188
  117.6 72.7 %all-gather.10.cloned.1.call-start = ((), (), s32[]{:S(2)}) async-start(), calls=%async_computation.2 | async-start | bytes 2359296 | tf_op jit(solution)/shard_map/all_gather | solution.py:44
  135.4 0.9 copy-start.1
  181.6 13.2 %copy-start.2 = (f32[1536,128]{0,1:T(8,128)S(1)}, f32[1536,128]{0,1:T(8,128)}, u32[]{:S(2)}) copy-start(f32[1536,128]{0,1:T(8,128)} %copy-done.1) | copy-start | bytes 2359300
Sparse Core Ops, SparseCore 0:
  10.2 63.1 all-gather.5
  117.7 8.3 all-gather.7
  181.8 8.4 all-gather.9
